TPU v7x, 32 devices: a whole 2x2x4 slice. The times are simulated.
32 devices in a mesh: row: 8 (over y, x, core), col: 4 (over z).
Axes of the slice: x: 2, y: 2, z: 4, core: 2. Of those that a mesh axis runs over, the one named last changes fastest.
Arguments:
- final_amp: bfloat16 [8, 32, 128, 440], P('row', 'col'), may hold values from -0.19921875 to 0.19921875
- initial_amp: bfloat16 [4, 32, 128, 440], P('col', 'row'), may hold values from -0.19921875 to 0.19921875
- pair_final: int32 [8, 4, 128], P('row', 'col'), may hold values from 0 to 31
- pair_initial: int32 [8, 4, 128], P('row', 'col'), may hold values from 0 to 31
- map_final: int32 [8, 32, 440], P('row', 'col'), may hold values from 0 to 439, each once within a row
- map_initial: int32 [4, 32, 440], P('col', 'row'), may hold values from 0 to 439, each once within a row
- counts: int32 [8, 4], P('row', 'col'), may hold values from 16 to 128, as said below
Outputs:
- density: float32 [440, 440], replicated
Inputs may be any that keep to these rules, and one draw needn't show every extreme that they name: `counts`: slots at or past a cell's count are ignored. Exactly one cell of every draw has 128 live slots.
All inputs are finite; a program needn't handle non-finite values.
Results may differ from a plain program's by a relative error of at most 0.0003.
Values may be sent and summed in bfloat16 or wider, within the bound.
A program may use at most 64 MiB of HBM per device.

v0:
```python
import functools

import jax
import jax.numpy as jnp
from jax import lax
from jax.experimental import pallas as pl
from jax.experimental.pallas import tpu as pltpu
from jax.sharding import PartitionSpec as P

MESH = pl.DeviceIdType.MESH
UNROLL = 8
CHUNKS = 3
LANES = 128


def flip(value, bit):
    return value + bit - 2 * bit * lax.rem(lax.div(value, bit), 2)


def flip_many(value, mask):
    bit = 1
    while bit <= mask:
        if mask & bit:
            value = flip(value, bit)
        bit *= 2
    return value


def relay_plan(rows):
    bits = []
    bit = 2
    while bit < rows:
        bits.append(bit)
        bit *= 2
    plans = []
    for order in (bits, bits[::-1]):
        diffs = [(0, 0)]
        for position, bit in enumerate(order):
            diffs += [(diff | bit, position + 1) for diff, _ in list(diffs)]
        plans.append((order, diffs))
    return plans


def permute(block, stored):
    orbitals = block.shape[0]
    chosen = lax.broadcasted_iota(jnp.int32, (orbitals, orbitals), 1) == stored
    onehot = jnp.where(chosen, 1.0, 0.0).astype(jnp.bfloat16)
    return jnp.dot(onehot, block, preferred_element_type=jnp.float32).astype(jnp.bfloat16)


def spread_kernel(rows, cols, fin_ref, ini_ref, fmap_ref, imap_ref, pf_ref, pi_ref, count_ref, f_all, i_all, l_all,
                  list_ref, f_own, i_own, zero, local_sem, send_sem, recv_sem, zsend, zrecv, fsend, frecv, lsend, lrecv):
    r = lax.axis_index("row")
    c = lax.axis_index("col")
    groups = cols // 2
    own_i = ini_ref.shape[1]
    own_f = fin_ref.shape[1]
    half = own_i // 2
    plans = relay_plan(rows)

    barrier = pltpu.get_barrier_semaphore()
    peers = []
    bit = 1
    while bit < rows:
        peers.append((flip(r, bit), c))
        bit *= 2
    peers += [(r, flip_many(c, mask)) for mask in [1] + [2 * g for g in range(1, groups)]]
    for peer in peers:
        pl.semaphore_signal(barrier, inc=1, device_id=peer, device_id_type=MESH)

    list_ref[0:1] = pf_ref[0]
    list_ref[1:2] = pi_ref[0]
    list_ref[2:8] = jnp.full((6, list_ref.shape[1]), count_ref[0, 0], jnp.int32)
    stored = imap_ref[0].T
    for j in range(own_i):
        i_own[j] = permute(ini_ref[0, j], stored[:, j:j + 1])
    pl.semaphore_wait(barrier, len(peers))

    sent = []

    def remote(src, dst, ssem, rsem, peer):
        copy = pltpu.make_async_remote_copy(src_ref=src, dst_ref=dst, send_sem=ssem, recv_sem=rsem,
                                            device_id=peer, device_id_type=MESH)
        copy.start()
        sent.append(copy)

    def part(h):
        return pl.ds(h * half, half)

    used = {}

    def forward(g, h, diff, position, src):
        order, _ = plans[h]
        targets = order[position:] + [1]
        for bit in targets:
            k = used.setdefault((g, h), 0)
            used[(g, h)] = k + 1
            remote(src, i_all.at[g, diff ^ bit, part(h)], send_sem.at[g, h, k], recv_sem.at[g, h, diff ^ bit],
                   (flip(r, bit), c))

    for h in range(2):
        for g in range(1, groups):
            remote(i_own.at[part(h)], i_all.at[g, 0, part(h)], zsend.at[g, h], zrecv.at[g, h], (r, flip_many(c, 2 * g)))
        forward(0, h, 0, 0, i_own.at[part(h)])
    for g in range(1, groups):
        remote(list_ref, l_all.at[g], lsend.at[g], lrecv.at[g], (r, flip_many(c, 2 * g)))

    local = [pltpu.make_async_copy(i_own, i_all.at[0, 0], local_sem.at[0]),
             pltpu.make_async_copy(list_ref, l_all.at[0], local_sem.at[1])]
    zero[...] = jnp.zeros_like(zero)
    stored = fmap_ref[0].T
    for j in range(own_f):
        f_own[j] = permute(fin_ref[0, j], stored[:, j:j + 1])
    remote(f_own, f_all.at[pl.ds(own_f, own_f)], fsend, frecv, (r, flip(c, 1)))
    local += [pltpu.make_async_copy(f_own, f_all.at[pl.ds(0, own_f)], local_sem.at[2]),
              pltpu.make_async_copy(zero, f_all.at[2 * own_f], local_sem.at[3])]
    for copy in local:
        copy.start()

    def arrived(ref, ssem, rsem):
        pltpu.make_async_remote_copy(src_ref=ref, dst_ref=ref, send_sem=ssem, recv_sem=rsem,
                                     device_id=(flip(r, 1), c), device_id_type=MESH).wait_recv()

    def relay(g, h, diff, position):
        here = i_all.at[g, diff, part(h)]
        if diff == 0:
            arrived(here, zsend.at[g, h], zrecv.at[g, h])
        else:
            arrived(here, send_sem.at[g, h, 0], recv_sem.at[g, h, diff])
        forward(g, h, diff, position, here)

    longest = len(plans[0][1])
    for wave in range(groups + longest):
        for g in range(groups):
            index = wave - g + 1
            if g == 0 and index == 0:
                continue
            for h in range(2):
                if g > 0:
                    index = wave - g
                if 0 <= index < longest:
                    diff, position = plans[h][1][index]
                    if g == 0 and diff == 0:
                        continue
                    relay(g, h, diff, position)
    for g in range(groups):
        for h in range(2):
            for diff, _ in plans[h][1]:
                arrived(i_all.at[g, diff ^ 1, part(h)], send_sem.at[g, h, 0], recv_sem.at[g, h, diff ^ 1])
    for g in range(1, groups):
        arrived(l_all.at[g], lsend.at[g], lrecv.at[g])
    arrived(f_all.at[pl.ds(own_f, own_f)], fsend, frecv)
    for copy in sent:
        copy.wait_send()
    for copy in local:
        copy.wait()


def density_kernel(rows, cols, own_f, own_i, f_ref, i_ref, l_ref, out_ref, acc, list_f, list_i):
    r = lax.axis_index("row")
    c = lax.axis_index("col")
    groups = cols // 2
    total = jnp.int32(0)
    for g in range(groups):
        def collect(p, n):
            q = l_ref[g, 0, p]
            s = l_ref[g, 1, p]
            apart = lax.div(q, own_f) ^ c
            list_f[n] = apart * own_f + lax.rem(q, own_f)
            list_i[n] = (g * rows + (lax.div(s, own_i) ^ r)) * own_i + lax.rem(s, own_i)
            return n + jnp.where(apart < 2, 1, 0).astype(jnp.int32)

        total = lax.fori_loop(0, l_ref[g, 2, 0], collect, total)
    for k in range(UNROLL):
        list_f[total + k] = 2 * own_f
        list_i[total + k] = 0
    acc[...] = jnp.zeros_like(acc)

    def step(t, carry):
        first = t * UNROLL
        left = jnp.concatenate([f_ref[list_f[first + k]] for k in range(UNROLL)], axis=1)
        right = jnp.concatenate([i_ref[list_i[first + k]] for k in range(UNROLL)], axis=1)
        acc[...] += lax.dot_general(left, right, (((1,), (1,)), ((), ())), preferred_element_type=jnp.float32)
        return carry

    lax.fori_loop(0, lax.div(total + UNROLL - 1, UNROLL), step, 0)
    orb = acc.shape[0]
    for block, first in enumerate(range(0, orb, LANES)):
        width = min(LANES, orb - first)
        if width < LANES:
            out_ref[block * orb:, :] = jnp.zeros((out_ref.shape[0] - block * orb, LANES), jnp.float32)
        out_ref[block * orb:(block + 1) * orb, :width] = acc[:, first:first + width]
    tail = pl.cdiv(orb, LANES) * orb
    if tail < out_ref.shape[0]:
        out_ref[tail:, :] = jnp.zeros((out_ref.shape[0] - tail, LANES), jnp.float32)


def chunks(total, unit):
    units = total // unit
    count = min(CHUNKS, units)
    pieces = []
    base = 0
    for n in range(count):
        length = (units // count + (n < units % count)) * unit
        pieces.append((base, length))
        base += length
    return pieces


def reduce_kernel(rows, cols, part_ref, out_ref, acc, res, rbuf, zbuf,
                  rs_send, rs_recv, z_send, z_recv, g_send, g_recv, ag_send, ag_recv):
    r = lax.axis_index("row")
    c = lax.axis_index("col")
    orders = [[1] + order for order, _ in relay_plan(rows)]
    steps = len(orders[0])

    barrier = pltpu.get_barrier_semaphore()
    peers = [(flip(r, bit), c) for bit in orders[0]] + [(r, flip_many(c, mask)) for mask in range(1, cols)]
    for peer in peers:
        pl.semaphore_signal(barrier, inc=1, device_id=peer, device_id_type=MESH)
    pl.semaphore_wait(barrier, len(peers))

    sent = []

    def remote(src, dst, ssem, rsem, peer):
        copy = pltpu.make_async_remote_copy(src_ref=src, dst_ref=dst, send_sem=ssem, recv_sem=rsem,
                                            device_id=peer, device_id_type=MESH)
        copy.start()
        sent.append(copy)
        return copy

    def rows_at(first, size):
        return pl.ds(pl.multiple_of(first, 8), size)

    share = cols // 2

    def chain(n, base, length):
        half = length // 2
        start = [r * 0 + base, r * 0 + base + half]
        size = half
        used = base // 2
        for step in range(steps):
            size //= 2
            source = part_ref if step == 0 else acc
            copies = []
            for h in range(2):
                bit = orders[h][step]
                mine = lax.rem(lax.div(r, bit), 2)
                give = start[h] + (1 - mine) * size
                start[h] = start[h] + mine * size
                copies.append(remote(source.at[rows_at(give, size)], rbuf.at[h, pl.ds(used, size)],
                                     rs_send.at[n, h, step], rs_recv.at[n, h, step], (flip(r, bit), c)))
            yield
            for h in range(2):
                copies[h].wait_recv()
                keep = rows_at(start[h], size)
                acc[keep, :] = source[keep, :] + rbuf[h, used:used + size, :]
            used += size
        sub = size // share

        def band(k):
            return rows_at(start[0] + (start[1] - start[0]) * lax.div(k, share) + lax.rem(k, share) * sub, sub)

        own = band(c)
        copies = []
        for mask in range(1, cols):
            peer = flip_many(c, mask)
            copies.append(remote(acc.at[band(peer)], zbuf.at[n, mask - 1, pl.ds(0, sub)],
                                 z_send.at[n, mask], z_recv.at[n, mask], (r, peer)))
        yield
        value = acc[own, :]
        for mask in range(1, cols):
            copies[mask - 1].wait_recv()
            value = value + zbuf[n, mask - 1, :sub]
        res[own, :] = value
        copies = []
        for mask in range(1, cols):
            copies.append(remote(res.at[own], res.at[own], g_send.at[n, mask], g_recv.at[n, mask],
                                 (r, flip_many(c, mask))))
        yield
        for copy in copies:
            copy.wait_recv()
        for step in reversed(range(steps)):
            copies = []
            for h in range(2):
                bit = orders[h][step]
                here = res.at[rows_at(start[h], size)]
                copies.append(remote(here, here, ag_send.at[n, h, step], ag_recv.at[n, h, step], (flip(r, bit), c)))
            yield
            for h in range(2):
                copies[h].wait_recv()
                start[h] = start[h] - lax.rem(lax.div(r, orders[h][step]), 2) * size
            size *= 2

    chains = [chain(n, *piece) for n, piece in enumerate(chunks(part_ref.shape[0], 8 * rows * cols))]
    while chains:
        for link in list(chains):
            try:
                next(link)
            except StopIteration:
                chains.remove(link)
    orb = out_ref.shape[0]
    for block, first in enumerate(range(0, orb, LANES)):
        width = min(LANES, orb - first)
        out_ref[:, first:first + width] = res[block * orb:(block + 1) * orb, :width]
    for copy in sent:
        copy.wait_send()


def shards(rows, cols, final_amp, initial_amp, pair_final, pair_initial, map_final, map_initial, counts):
    own_f, blk, orb = final_amp.shape[1:]
    own_i = initial_amp.shape[1]
    slots = pair_final.shape[2]
    groups = cols // 2
    vmem = pl.BlockSpec(memory_space=pltpu.VMEM)
    hbm = pl.BlockSpec(memory_space=pl.ANY)
    dma = pltpu.SemaphoreType.DMA
    f_all, i_all, l_all = pl.pallas_call(
        functools.partial(spread_kernel, rows, cols),
        out_shape=(jax.ShapeDtypeStruct((2 * own_f + 1, orb, blk), jnp.bfloat16),
                   jax.ShapeDtypeStruct((groups, rows, own_i, orb, blk), jnp.bfloat16),
                   jax.ShapeDtypeStruct((groups, 8, slots), jnp.int32)),
        in_specs=[vmem] * 6 + [pl.BlockSpec(memory_space=pltpu.SMEM)],
        out_specs=(hbm, hbm, hbm),
        scratch_shapes=[pltpu.VMEM((8, slots), jnp.int32), pltpu.VMEM((own_f, orb, blk), jnp.bfloat16), pltpu.VMEM((own_i, orb, blk), jnp.bfloat16),
                        pltpu.VMEM((orb, blk), jnp.bfloat16),
                        dma((4,)), dma((groups, 2, rows)), dma((groups, 2, rows)),
                        dma((groups, 2)), dma((groups, 2)), dma, dma, dma((groups,)), dma((groups,))],
        compiler_params=pltpu.CompilerParams(collective_id=0, has_side_effects=True, vmem_limit_bytes=20 << 20),
    )(final_amp.swapaxes(2, 3), initial_amp.swapaxes(2, 3), map_final, map_initial, pair_final, pair_initial, counts)
    i_all = i_all.reshape(-1, orb, blk)
    unit = 8 * rows * cols
    total = pl.cdiv(pl.cdiv(orb, LANES) * orb, unit) * unit
    partial = pl.pallas_call(
        functools.partial(density_kernel, rows, cols, own_f, own_i),
        out_shape=jax.ShapeDtypeStruct((total, LANES), jnp.float32),
        in_specs=[vmem, vmem, pl.BlockSpec(memory_space=pltpu.SMEM)],
        out_specs=vmem,
        scratch_shapes=[pltpu.VMEM((orb, orb), jnp.float32)]
        + [pltpu.SMEM((groups * slots + UNROLL,), jnp.int32)] * 2,
        compiler_params=pltpu.CompilerParams(vmem_limit_bytes=20 << 20),
    )(f_all, i_all, l_all)
    pieces = chunks(total, unit)
    many = len(pieces)
    largest = pieces[0][1] // 2 // rows // (cols // 2)
    steps = rows.bit_length() - 1
    return pl.pallas_call(
        functools.partial(reduce_kernel, rows, cols),
        out_shape=jax.ShapeDtypeStruct((orb, orb), jnp.float32),
        in_specs=[vmem],
        out_specs=vmem,
        scratch_shapes=[pltpu.VMEM((total, LANES), jnp.float32), pltpu.VMEM((total, LANES), jnp.float32),
                        pltpu.VMEM((2, total // 2, LANES), jnp.float32),
                        pltpu.VMEM((many, cols - 1, largest, LANES), jnp.float32),
                        dma((many, 2, steps)), dma((many, 2, steps)), dma((many, cols)), dma((many, cols)),
                        dma((many, cols)), dma((many, cols)), dma((many, 2, steps)), dma((many, 2, steps))],
        compiler_params=pltpu.CompilerParams(collective_id=1, has_side_effects=True, vmem_limit_bytes=20 << 20),
    )(partial)


def solution(mesh):
    placed = (
        P("row", "col", None, None),
        P("col", "row", None, None),
        P("row", "col", None),
        P("row", "col", None),
        P("row", "col", None),
        P("col", "row", None),
        P("row", "col"),
    )
    body = functools.partial(shards, mesh.shape["row"], mesh.shape["col"])
    return jax.shard_map(body, mesh=mesh, in_specs=placed, out_specs=P(), check_vma=False)
```

profile of v0, /device:TPU:0, one launch (start us, length us, event | category | flops | bytes accessed | tf_op | source)
XLA Modules:
  0.0 82.2 jit_solution(18394912903152424339)
XLA Ops:
  0.7 0.0 copy-start
  0.7 1.2 %copy-done = bf16[1,8,128,440]{2,3,1,0:T(8,128)(2,1)S(1)} copy-done((bf16[1,8,128,440]{2,3,1,0:T(8,128)(2,1)S(1)}, bf16[1,8,128,440]{2,3,1,0:T(8,128)(2,1)}, u32[]{:S(2)}) %copy-start) | copy-done | bytes 901144
  1.8 0.0 copy-start.1
  1.8 1.0 %copy-done.1 = bf16[1,4,128,440]{2,3,1,0:T(8,128)(2,1)S(1)} copy-done((bf16[1,4,128,440]{2,3,1,0:T(8,128)(2,1)S(1)}, bf16[1,4,128,440]{2,3,1,0:T(8,128)(2,1)}, u32[]{:S(2)}) %copy-start.1) | copy-done | bytes 450584
  2.8 0.0 copy-start.2
  2.8 0.7 copy-done.2
  3.6 0.0 copy-start.3
  3.6 0.7 copy-done.3
  4.3 0.0 copy-start.4
  4.3 0.7 copy-done.4
  4.9 0.0 copy-start.5
  4.9 0.7 copy-done.5
  5.6 40.8 %shard_map.73 = (bf16[17,440,128]{2,1,0:T(8,128)(2,1)S(1)}, bf16[2,8,4,440,128]{4,3,2,1,0:T(8,128)(2,1)S(1)}, s32[2,8,128]{2,1,0:T(8,128)S(1)}) custom-call(bf16[1,8,440,128]{3,2,1,0:T(8,128)(2,1)S(1)} %bitcast.4, bf16[1,4,440,128]{3,2,1,0:T(8,128)(2,1)S(1)} %bitcast.5, s32[1,8,440]{2,1,0:T(8,128)S(1)} %copy-done.2, s32[1,4,440]{2,1,0:T(4,128)S(1)} %copy-done.3, ...), custom_call_target="tpu_custom_call" | custom-call | tf_op jit(solution)/shard_map/pallas_call | solution.py:318
  46.3 5.2 %shard_map.74.part_ref = f32[1792,128]{1,0:T(8,128)S(1)} custom-call(bf16[17,440,128]{2,1,0:T(8,128)(2,1)S(1)} %get-tuple-element.8.f_ref, bf16[64,440,128]{2,1,0:T(8,128)(2,1)S(1)} %bitcast.3, s32[2,8,128]{2,1,0:T(8,128)S(1)} %get-tuple-element.10.l_ref), custom_call_target="tpu_custom_call" | custom-call | tf_op jit(solution)/shard_map/pallas_call | solution.py:334
  51.6 29.6 %shard_map.75 = f32[440,440]{1,0:T(8,128)S(1)} custom-call(f32[1792,128]{1,0:T(8,128)S(1)} %shard_map.74.part_ref), custom_call_target="tpu_custom_call" | custom-call | tf_op jit(solution)/shard_map/pallas_call | solution.py:347
  81.2 0.9 %copy.10 = f32[440,440]{1,0:T(8,128)} copy(f32[440,440]{1,0:T(8,128)S(1)} %shard_map.75) | data formatting | bytes 1548800
Async XLA Ops:
  0.7 1.2 %copy-start = (bf16[1,8,128,440]{2,3,1,0:T(8,128)(2,1)S(1)}, bf16[1,8,128,440]{2,3,1,0:T(8,128)(2,1)}, u32[]{:S(2)}) copy-start(bf16[1,8,128,440]{2,3,1,0:T(8,128)(2,1)} %param.7) | copy-start | bytes 2703364
  1.8 1.0 %copy-start.1 = (bf16[1,4,128,440]{2,3,1,0:T(8,128)(2,1)S(1)}, bf16[1,4,128,440]{2,3,1,0:T(8,128)(2,1)}, u32[]{:S(2)}) copy-start(bf16[1,4,128,440]{2,3,1,0:T(8,128)(2,1)} %param.8) | copy-start | bytes 1351684
  2.8 0.7 copy-start.2
  3.6 0.7 copy-start.3
  4.3 0.7 copy-start.4
  4.9 0.7 copy-start.5
where the time goes:
time: 83.3 us; the launch traced here: 82.2 us
  Pallas kernels  75.6 us (91%)
  local copies, waits for them, and re-layouts  5.82 us (7%)
    pallas_call x1, Pallas kernels, shards(): pl.pallas_call(functools.partial(spread_kernel, rows, cols), out_shape=(j...  40.8 us
    pallas_call x1, Pallas kernels, shards(): pl.pallas_call(functools.partial(reduce_kernel, rows, cols), out_shape=ja...  29.6 us
    unnamed x13, local copies, waits for them, and re-layouts  5.82 us
    pallas_call x1, Pallas kernels, shards(): pl.pallas_call(functools.partial(density_kernel, rows, cols, own_f, own_i...  5.24 us

commit v1 on v0

--- a/solution.py
+++ b/solution.py
@@ -9,7 +9,7 @@
 
 MESH = pl.DeviceIdType.MESH
 UNROLL = 8
-CHUNKS = 3
+CHUNKS = 4
 LANES = 128
 
 
@@ -48,11 +48,16 @@
     return jnp.dot(onehot, block, preferred_element_type=jnp.float32).astype(jnp.bfloat16)
 
 
-def spread_kernel(rows, cols, fin_ref, ini_ref, fmap_ref, imap_ref, pf_ref, pi_ref, count_ref, f_all, i_all, l_all,
-                  list_ref, f_own, i_own, zero, local_sem, send_sem, recv_sem, zsend, zrecv, fsend, frecv, lsend, lrecv):
+def spread_kernel(rows, cols, fin_hbm, ini_hbm, fmap_hbm, imap_hbm, pf_hbm, pi_hbm, count_ref, f_all, i_all, l_all,
+                  fin_ref, ini_ref, fmap_ref, imap_ref, pf_ref, pi_ref, load_sem, list_ref, f_own, i_own, zero, local_sem, send_sem, recv_sem, zsend, zrecv, fsend, frecv, lsend, lrecv):
     r = lax.axis_index("row")
     c = lax.axis_index("col")
     groups = cols // 2
+    pairs = ((imap_hbm, imap_ref), (ini_hbm, ini_ref), (pf_hbm, pf_ref), (pi_hbm, pi_ref),
+             (fmap_hbm, fmap_ref), (fin_hbm, fin_ref))
+    loads = [pltpu.make_async_copy(src, dst, load_sem.at[n]) for n, (src, dst) in enumerate(pairs)]
+    for load in loads:
+        load.start()
     own_i = ini_ref.shape[1]
     own_f = fin_ref.shape[1]
     half = own_i // 2
@@ -68,6 +73,8 @@
     for peer in peers:
         pl.semaphore_signal(barrier, inc=1, device_id=peer, device_id_type=MESH)
 
+    for load in loads[:4]:
+        load.wait()
     list_ref[0:1] = pf_ref[0]
     list_ref[1:2] = pi_ref[0]
     list_ref[2:8] = jnp.full((6, list_ref.shape[1]), count_ref[0, 0], jnp.int32)
@@ -108,6 +115,8 @@
     local = [pltpu.make_async_copy(i_own, i_all.at[0, 0], local_sem.at[0]),
              pltpu.make_async_copy(list_ref, l_all.at[0], local_sem.at[1])]
     zero[...] = jnp.zeros_like(zero)
+    for load in loads[4:]:
+        load.wait()
     stored = fmap_ref[0].T
     for j in range(own_f):
         f_own[j] = permute(fin_ref[0, j], stored[:, j:j + 1])
@@ -156,7 +165,10 @@
         copy.wait()
 
 
-def density_kernel(rows, cols, own_f, own_i, f_ref, i_ref, l_ref, out_ref, acc, list_f, list_i):
+def density_kernel(rows, cols, own_f, own_i, f_hbm, i_hbm, l_ref, out_ref, f_ref, i_ref, load_sem, acc, list_f, list_i):
+    loads = [pltpu.make_async_copy(i_hbm, i_ref, load_sem.at[0]), pltpu.make_async_copy(f_hbm, f_ref, load_sem.at[1])]
+    for load in loads:
+        load.start()
     r = lax.axis_index("row")
     c = lax.axis_index("col")
     groups = cols // 2
@@ -175,6 +187,8 @@
         list_f[total + k] = 2 * own_f
         list_i[total + k] = 0
     acc[...] = jnp.zeros_like(acc)
+    for load in loads:
+        load.wait()
 
     def step(t, carry):
         first = t * UNROLL
@@ -320,13 +334,16 @@
         out_shape=(jax.ShapeDtypeStruct((2 * own_f + 1, orb, blk), jnp.bfloat16),
                    jax.ShapeDtypeStruct((groups, rows, own_i, orb, blk), jnp.bfloat16),
                    jax.ShapeDtypeStruct((groups, 8, slots), jnp.int32)),
-        in_specs=[vmem] * 6 + [pl.BlockSpec(memory_space=pltpu.SMEM)],
+        in_specs=[pl.BlockSpec(memory_space=pltpu.HBM)] * 6 + [pl.BlockSpec(memory_space=pltpu.SMEM)],
         out_specs=(hbm, hbm, hbm),
-        scratch_shapes=[pltpu.VMEM((8, slots), jnp.int32), pltpu.VMEM((own_f, orb, blk), jnp.bfloat16), pltpu.VMEM((own_i, orb, blk), jnp.bfloat16),
+        scratch_shapes=[pltpu.VMEM((1, own_f, orb, blk), jnp.bfloat16), pltpu.VMEM((1, own_i, orb, blk), jnp.bfloat16),
+                        pltpu.VMEM(map_final.shape, jnp.int32), pltpu.VMEM(map_initial.shape, jnp.int32),
+                        pltpu.VMEM(pair_final.shape, jnp.int32), pltpu.VMEM(pair_initial.shape, jnp.int32),
+                        dma((6,)), pltpu.VMEM((8, slots), jnp.int32), pltpu.VMEM((own_f, orb, blk), jnp.bfloat16), pltpu.VMEM((own_i, orb, blk), jnp.bfloat16),
                         pltpu.VMEM((orb, blk), jnp.bfloat16),
                         dma((4,)), dma((groups, 2, rows)), dma((groups, 2, rows)),
                         dma((groups, 2)), dma((groups, 2)), dma, dma, dma((groups,)), dma((groups,))],
-        compiler_params=pltpu.CompilerParams(collective_id=0, has_side_effects=True, vmem_limit_bytes=20 << 20),
+        compiler_params=pltpu.CompilerParams(collective_id=0, has_side_effects=True, vmem_limit_bytes=56 << 20),
     )(final_amp.swapaxes(2, 3), initial_amp.swapaxes(2, 3), map_final, map_initial, pair_final, pair_initial, counts)
     i_all = i_all.reshape(-1, orb, blk)
     unit = 8 * rows * cols
@@ -334,11 +351,12 @@
     partial = pl.pallas_call(
         functools.partial(density_kernel, rows, cols, own_f, own_i),
         out_shape=jax.ShapeDtypeStruct((total, LANES), jnp.float32),
-        in_specs=[vmem, vmem, pl.BlockSpec(memory_space=pltpu.SMEM)],
+        in_specs=[pl.BlockSpec(memory_space=pltpu.HBM)] * 2 + [pl.BlockSpec(memory_space=pltpu.SMEM)],
         out_specs=vmem,
-        scratch_shapes=[pltpu.VMEM((orb, orb), jnp.float32)]
+        scratch_shapes=[pltpu.VMEM(f_all.shape, jnp.bfloat16), pltpu.VMEM(i_all.shape, jnp.bfloat16), dma((2,)),
+                        pltpu.VMEM((orb, orb), jnp.float32)]
         + [pltpu.SMEM((groups * slots + UNROLL,), jnp.int32)] * 2,
-        compiler_params=pltpu.CompilerParams(vmem_limit_bytes=20 << 20),
+        compiler_params=pltpu.CompilerParams(vmem_limit_bytes=56 << 20),
     )(f_all, i_all, l_all)
     pieces = chunks(total, unit)
     many = len(pieces)

time: 83.3 us -> 83 us (level); the launches traced: 82.2 us -> 83.1 us
  Pallas kernels: 75.6 us -> 80.3 us
  local copies, waits for them, and re-layouts: 5.82 us -> 2.09 us
    pallas_call x1, Pallas kernels: 5.24 us -> 9.42 us  [shards(): pl.pallas_call(functools.partial(density_kernel, rows, cols, own_f, own_i...]
    unnamed x13 -> x3, local copies, waits for them, and re-layouts: 5.82 us -> 2.09 us
    pallas_call x1, Pallas kernels: 40.8 us -> 42.5 us  [shards(): pl.pallas_call(functools.partial(spread_kernel, rows, cols), out_shape=(j...]
    pallas_call x1, Pallas kernels: 29.6 us -> 28.3 us  [shards(): pl.pallas_call(functools.partial(reduce_kernel, rows, cols), out_shape=ja...]
where the time goes in v1:
time: 83 us; the launch traced here: 83.1 us
  Pallas kernels  80.3 us (97%)
  local copies, waits for them, and re-layouts  2.09 us (3%)
    pallas_call x1, Pallas kernels, shards(): pl.pallas_call(functools.partial(spread_kernel, rows, cols), out_shape=(j...  42.5 us
    pallas_call x1, Pallas kernels, shards(): pl.pallas_call(functools.partial(reduce_kernel, rows, cols), out_shape=ja...  28.3 us
    pallas_call x1, Pallas kernels, shards(): pl.pallas_call(functools.partial(density_kernel, rows, cols, own_f, own_i...  9.42 us
    unnamed x3, local copies, waits for them, and re-layouts  2.09 us

profile of v1, /device:TPU:0, one launch (start us, length us, event | category | flops | bytes accessed | tf_op | source)
XLA Modules:
  0.0 83.1 jit_solution(1925365168506385133)
XLA Ops:
  0.7 42.5 %shard_map.73 = (bf16[17,440,128]{2,1,0:T(8,128)(2,1)}, bf16[2,8,4,440,128]{4,3,2,1,0:T(8,128)(2,1)}, s32[2,8,128]{2,1,0:T(8,128)}) custom-call(bf16[1,8,440,128]{3,2,1,0:T(8,128)(2,1)} %bitcast.4, bf16[1,4,440,128]{3,2,1,0:T(8,128)(2,1)} %bitcast.5, s32[1,8,440]{2,1,0:T(8,128)} %fmap_hbm.1, s32[1,4,440]{2,1,0:T(4,128)} %imap_hbm.1, s32[1,1,128]{2,1,0:T(1,128)} %pf_hbm.1, ...), custom_call_target="tpu_custom_call" | custom-call | tf_op jit(solution)/shard_map/pallas_call | solution.py:332
  43.2 9.4 %shard_map.74.part_ref = f32[1792,128]{1,0:T(8,128)} custom-call(bf16[17,440,128]{2,1,0:T(8,128)(2,1)} %get-tuple-element.8.f_hbm, bf16[64,440,128]{2,1,0:T(8,128)(2,1)} %bitcast.3, s32[2,8,128]{2,1,0:T(8,128)} %get-tuple-element.10.l_ref), custom_call_target="tpu_custom_call" | custom-call | tf_op jit(solution)/shard_map/pallas_call | solution.py:351
  52.6 0.0 copy-start
  52.6 1.2 %copy-done = f32[1792,128]{1,0:T(8,128)S(1)} copy-done((f32[1792,128]{1,0:T(8,128)S(1)}, f32[1792,128]{1,0:T(8,128)}, u32[]{:S(2)}) %copy-start) | copy-done | bytes 917528
  53.8 28.3 %shard_map.75 = f32[440,440]{1,0:T(8,128)S(1)} custom-call(f32[1792,128]{1,0:T(8,128)S(1)} %copy-done), custom_call_target="tpu_custom_call" | custom-call | tf_op jit(solution)/shard_map/pallas_call | solution.py:365
  82.2 0.9 %copy.10 = f32[440,440]{1,0:T(8,128)} copy(f32[440,440]{1,0:T(8,128)S(1)} %shard_map.75) | data formatting | bytes 1548800
Async XLA Ops:
  52.6 1.2 %copy-start = (f32[1792,128]{1,0:T(8,128)S(1)}, f32[1792,128]{1,0:T(8,128)}, u32[]{:S(2)}) copy-start(f32[1792,128]{1,0:T(8,128)} %shard_map.74.part_ref) | copy-start | bytes 2752516
